TPU v7x, 512 devices: a whole 4x8x8 slice. The times are simulated.
512 devices in a mesh: mirror: 2 (over y_hi), rows: 64 (over z, y_lo, core), cols: 4 (over x).
Axes of the slice: x: 4, y: 8 (y_hi: 2, y_lo: 4; y = y_hi * 4 + y_lo), z: 8, core: 2. Of those that a mesh axis runs over, the one named last changes fastest.
Arguments:
- currents: bfloat16 [16, 131072], P(None, ('mirror', 'rows')), may hold values from -6 to 6
- right_side: float32 [16, 131072], P(None, ('mirror', 'rows', 'cols')), may hold values from -6 to 6
- geometry: float32 [4, 65536], replicated, may hold values from 0 to 4, as said below
Outputs:
- residual: float32 [16, 131072], P(None, ('mirror', 'rows', 'cols'))
- krylov_image: float32 [16, 131072], P(None, ('mirror', 'rows', 'cols'))
Inputs may be any that keep to these rules, and one draw needn't show every extreme that they name: `geometry`: rows are x in [0, 1], y in [0.05, 0.45], z in [0, 4] and a size in [0.003, 0.03].
All inputs are finite; a program needn't handle non-finite values.
Results may differ from a plain program's by a relative error of at most 0.0024.
Values may be sent and summed in bfloat16 or wider, within the bound.
A program may use at most 64 MiB of HBM per device.

v0:
```python
import math

import jax
import jax.numpy as jnp
from jax import lax
from jax.sharding import PartitionSpec as P


def partner_2(block, axis, apart):
    count = lax.axis_size(axis)
    route = []
    for low in range(count):
        high = low | 1 << apart
        if high != low and high < count:
            route += [(low, high), (high, low)]
    return lax.ppermute(block, axis, route)


def kernel_block(row_geo, col_geo, reflect, scaling):
    diff_x = row_geo[0][:, None] - col_geo[0][None, :]
    diff_y = row_geo[1][:, None] - reflect * col_geo[1][None, :]
    diff_z = row_geo[2][:, None] - col_geo[2][None, :]
    spread = (row_geo[3] * row_geo[3])[:, None] + (col_geo[3] * col_geo[3])[None, :]
    squared = diff_x * diff_x + diff_y * diff_y + diff_z * diff_z + spread
    return (scaling / jnp.sqrt(squared)).astype(jnp.bfloat16)


def forward(stacked, source_geo, target_geo, reflect, scaling):
    excite = stacked.shape[1]
    target_len = target_geo.shape[1]
    block_len = min(1024, target_len)
    zero_sums = jnp.zeros((excite, 2, target_len), jnp.float32)

    def advance(position, totals):
        offset = position * block_len
        geo_part = lax.dynamic_slice_in_dim(target_geo, offset, block_len, 1)
        kernel_tile = kernel_block(source_geo, geo_part, reflect, scaling)
        partial_value = jnp.einsum(
            "hrs,st->rht", stacked, kernel_tile, preferred_element_type=jnp.float32
        )
        return lax.dynamic_update_slice_in_dim(totals, partial_value, offset, 2)

    totals = lax.fori_loop(0, target_len // block_len, advance, zero_sums)
    return totals.reshape(excite, 2 * target_len)


def on_device(currents, right_side, geometry):
    half_index = lax.axis_index("mirror")
    row_index = lax.axis_index("rows")
    col_index = lax.axis_index("cols")
    row_count = lax.axis_size("rows")
    col_count = lax.axis_size("cols")
    block_cells = currents.shape[1]
    piece_len = block_cells // col_count
    half_cells = geometry.shape[1]
    scaling = 1.0 / math.sqrt(2 * half_cells)
    reflect = 1.0 - 2.0 * half_index.astype(jnp.float32)
    block_geo = lax.dynamic_slice_in_dim(geometry, row_index * block_cells, block_cells, 1)
    strided_geo = lax.dynamic_index_in_dim(
        geometry.reshape(4, row_count, col_count, piece_len), col_index, 2, False
    ).reshape(4, row_count * piece_len)
    partner = partner_2(currents, "mirror", 0)
    partial_value = forward(
        jnp.stack([currents, partner]), block_geo, strided_geo, reflect, scaling
    )
    voltage = lax.psum_scatter(partial_value, ("mirror", "rows"), scatter_dimension=1, tiled=True)
    residual = right_side - voltage
    residual_b = residual.astype(jnp.bfloat16)
    block_cur = lax.all_gather(residual_b, "cols", axis=1, tiled=True)
    partner_block = partner_2(block_cur, "mirror", 0)
    partial_two = forward(
        jnp.stack([block_cur, partner_block]), block_geo, strided_geo, reflect, scaling
    )
    krylov_image = lax.psum_scatter(
        partial_two, ("mirror", "rows"), scatter_dimension=1, tiled=True
    )
    return (residual, krylov_image)


def solution(mesh):
    placed = (P(None, ("mirror", "rows")), P(None, ("mirror", "rows", "cols")), P())
    return jax.shard_map(
        on_device,
        mesh=mesh,
        in_specs=placed,
        out_specs=(P(None, ("mirror", "rows", "cols")), P(None, ("mirror", "rows", "cols"))),
        check_vma=False,
    )
```

profile of v0, /device:TPU:255, one launch (start us, length us, event | category | flops | bytes accessed | tf_op | source)
XLA Modules:
  0.0 1218.5 jit_solution(13401681409278147913)
XLA Ops:
  7.2 4.4 collective-permute-start
  13.2 2.1 reshape.43
  17.2 34.5 %while.28 = (s32[]{:T(128)}, f32[16,2,16384]{2,1,0:T(2,128)S(1)}, f32[4,1024]{1,0:T(4,128)S(1)}, f32[4,16384]{1,0:T(4,128)S(1)}, f32[]{:T(128)}, /*index=5*/f32[...) while((s32[]{:T(128)}, f32[16,2,16384]{2,1,0:T(2,128)S(1)}, ...), condition=%wide.region_1.2_spmd, body=%wide.region_0.1_spmd.sunk | while | flops 79693832 | bytes 549103 | solution.py:43
  21.6 1.9 fusion.28
  23.8 1.9 fusion.28
  25.9 1.9 fusion.28
  28.1 1.9 fusion.28
  30.2 1.9 fusion.28
  34.5 1.9 fusion.28
  36.7 1.9 fusion.28
  38.8 1.9 fusion.28
  41.0 1.9 fusion.28
  43.2 1.9 fusion.28
  47.5 1.9 fusion.28
  49.6 1.9 fusion.28
  51.7 2.6 copy.14
  54.3 551.9 %reduce-scatter.3.cloned.1.call-done = f32[16,256]{1,0:T(8,128)} async-done(((f32[16,32768]{1,0:T(8,128)}), f32[16,256]{1,0:T(8,128)}) %reduce-scatter.3.cloned.1.call-update) | async-done | bytes 16400 | tf_op jit(solution)/shard_map/reduce_scatter | solution.py:66
  607.5 9.0 all_gather.3
  616.5 1.9 collective-permute-start.1
  618.5 6.6 collective-permute-done.1
  625.9 34.5 %while.29 = (s32[]{:T(128)}, f32[16,2,16384]{2,1,0:T(2,128)S(1)}, f32[4,1024]{1,0:T(4,128)S(1)}, f32[4,16384]{1,0:T(4,128)S(1)}, f32[]{:T(128)}, /*index=5*/f32[...) while((s32[]{:T(128)}, f32[16,2,16384]{2,1,0:T(2,128)S(1)}, ...), condition=%wide.region_4.5_spmd, body=%wide.region_3.4_spmd.sunk | while | flops 79693832 | bytes 549103 | solution.py:43
  626.0 1.9 fusion.31
  660.4 2.6 copy.15
  663.0 548.7 %reduce-scatter.5.cloned.1.call-done = f32[16,256]{1,0:T(8,128)} async-done(((f32[16,32768]{1,0:T(8,128)}), f32[16,256]{1,0:T(8,128)}) %reduce-scatter.5.cloned.1.call-update) | async-done | bytes 16400 | tf_op jit(solution)/shard_map/reduce_scatter | solution.py:74
  (101 shorter events, 48.8 us)
Async XLA Ops:
  7.2 9.2 copy-start
  7.2 599.0 %reduce-scatter.3.cloned.1.call-start = ((), (), s32[]{:S(2)}) async-start(), calls=%async_computation.2 | async-start | bytes 2113536 | tf_op jit(solution)/shard_map/reduce_scatter | solution.py:66
  7.2 9.1 collective-permute-start
  54.2 552.0 %copy-start.1 = (f32[16,256]{1,0:T(8,128)S(1)}, f32[16,256]{1,0:T(8,128)}, u32[]{:S(2)}) copy-start(f32[16,256]{1,0:T(8,128)} %param.8) | copy-start | bytes 49156
  54.3 1157.4 %reduce-scatter.5.cloned.1.call-start = ((), (), s32[]{:S(2)}) async-start(), calls=%async_computation.3 | async-start | bytes 2113536 | tf_op jit(solution)/shard_map/reduce_scatter | solution.py:74
  616.5 8.6 collective-permute-start.1
Sparse Core Ops, SparseCore 0:
  54.4 551.7 reduce-scatter.2
  663.1 548.4 reduce-scatter.4
where the time goes:
time: 1220 us
  waiting for transfers between devices  1110 us (91%)
  matrix products  60.7 us (5%)
  local copies, waits for them, and re-layouts  14.3 us (1%)
  between operations  14.1 us (1%)
    reduce_scatter x1, waiting for transfers between devices, on_device(): lax.psum_scatter(partial_value, ('mirror', 'rows'), scatter_dimension=1,...  552 us
    reduce_scatter x1, waiting for transfers between devices, on_device(): lax.psum_scatter(partial_two, ('mirror', 'rows'), scatter_dimension=1, ti...  549 us
    dot_general x32, matrix products, advance(): jnp.einsum('hrs,st->rht', stacked, kernel_tile, preferred_element_type=jn...  60.7 us
  transfers between devices with their start and end apart: 4, of which 4 were waited for; matrix products, arithmetic and copies ran while one was open for 0% of the time, Pallas kernels for 0%

commit v1 on v0

v1 whole, which is shorter than its diff:
```python
import functools

import jax
import jax.numpy as jnp
from jax import lax
from jax.experimental import pallas as pl
from jax.experimental.pallas import tpu as pltpu
from jax.sharding import PartitionSpec as P

MESH = pl.DeviceIdType.MESH
F32, BF16 = jnp.float32, jnp.bfloat16
HALF = 65536
RHS = 16
PIECE = 256
SOURCES = 4096
TARGETS = 2048
PIECES = SOURCES // PIECE
BLOCKS = TARGETS // PIECE
TERMS = 32
SQUARE = 2.0**17
ROOT = 2.0**8.5
CHUNK = 256
SENDERS = 16


def split3(value):
    high = value.astype(BF16).astype(F32)
    rest = value - high
    middle = rest.astype(BF16).astype(F32)
    return high, middle, (rest - middle).astype(BF16).astype(F32)


def store_terms(geo, terms, source):
    across = geo[0:1, :] - 0.5
    height = geo[1:2, :] - 0.25
    size = geo[3:4, :]
    own = across * across + height * height + size * size
    xs, ys, qs = split3(across), split3(height), split3(own)
    one = jnp.ones_like(across)
    if source:
        zs = split3(geo[2:3, :] - 2.0)
        rows = [v[i] for v in (xs, ys) for i in (0, 0, 1, 0, 2, 1)]
        rows += [*qs, one, one, one, *zs]
    else:
        rows = [v[i] * (-2.0 * SQUARE) for v in (xs, ys) for i in (0, 1, 0, 2, 0, 1)]
        rows += [one * SQUARE] * 3 + [v * SQUARE for v in qs]
    for k in range(TERMS):
        terms[k : k + 1, :] = rows[k] if k < len(rows) else jnp.zeros_like(across)


def kernel(
    cur_ref, right_ref, geo_ref, res_ref, img_ref,
    a_ref, b_ref, gs_ref, gt_ref, fs_ref, ft_ref, l_ref, r_ref, zb_ref, yb_ref, zt_ref,
    own_ref, j_ref, v_ref, p_ref,
    geo_sem, gather_send, gather_recv, part_send, part_recv,
):
    mirror = lax.axis_index("mirror")
    row = lax.axis_index("rows")
    col = lax.axis_index("cols")
    core = row % 2
    home = row // 32
    slot = (row % 32) // 2
    area = row // 2
    me = mirror * 8 + core * 4 + col
    mine = core * 4 + col

    barrier = pltpu.get_barrier_semaphore()

    def greet_source(k, carry):
        for half in range(2):
            other = mirror * 32 + 2 * k + core

            @pl.when(jnp.logical_or(other != row, mirror != half))
            def _():
                pl.semaphore_signal(barrier, inc=1, device_id=(half, other, col), device_id_type=MESH)

        return carry

    lax.fori_loop(0, PIECES, greet_source, 0)

    def greet_part(k, carry):
        @pl.when(k != me)
        def _():
            pl.semaphore_signal(
                barrier, inc=1, device_id=(k // 8, area * 2 + (k // 4) % 2, k % 4), device_id_type=MESH
            )

        return carry

    lax.fori_loop(0, SENDERS, greet_part, 0)

    def source_geo(k, carry):
        start = pl.multiple_of((mirror * 32 + 2 * k + core) * 1024 + col * PIECE, PIECE)
        into = pl.multiple_of(k * PIECE, PIECE)
        pltpu.make_async_copy(
            geo_ref.at[:, pl.ds(start, PIECE)], gs_ref.at[:, pl.ds(into, PIECE)], geo_sem.at[0]
        ).start()
        return carry

    lax.fori_loop(0, PIECES, source_geo, 0)
    first = pl.multiple_of(area * TARGETS, TARGETS)
    target_geo = pltpu.make_async_copy(geo_ref.at[:, pl.ds(first, TARGETS)], gt_ref, geo_sem.at[1])
    target_geo.start()
    own_ref[0] = cur_ref[:, pl.ds(pl.multiple_of(col * PIECE, PIECE), PIECE)]
    pltpu.make_async_copy(geo_ref.at[:, pl.ds(0, SOURCES)], gs_ref, geo_sem.at[0]).wait()
    target_geo.wait()

    def gather_copy(which, j):
        into = pl.multiple_of(slot * PIECE, PIECE)
        return pltpu.make_async_remote_copy(
            src_ref=own_ref.at[which],
            dst_ref=j_ref.at[which, pl.ds(pl.multiple_of(mirror * RHS, RHS), RHS), pl.ds(into, PIECE)],
            send_sem=gather_send.at[which, j],
            recv_sem=gather_recv.at[which],
            device_id=(home, 2 * j + core, col),
            device_id_type=MESH,
        )

    def is_self(j):
        return jnp.logical_and(home == mirror, 2 * j + core == row)

    def gather_start(which):
        def send(i, carry):
            j = (area + i) % 32

            @pl.when(jnp.logical_not(is_self(j)))
            def _():
                gather_copy(which, j).start()

            @pl.when(is_self(j))
            def _():
                into = pl.multiple_of(slot * PIECE, PIECE)
                pltpu.make_async_copy(
                    own_ref.at[which],
                    j_ref.at[which, pl.ds(pl.multiple_of(mirror * RHS, RHS), RHS), pl.ds(into, PIECE)],
                    gather_recv.at[which],
                ).start()

            return carry

        lax.fori_loop(0, 32, send, 0)

    def gather_wait(which):
        pltpu.make_async_copy(j_ref.at[which], j_ref.at[which], gather_recv.at[which]).wait()

    def part_copy(which, half, block):
        start = pl.multiple_of(block * PIECE, PIECE)
        return pltpu.make_async_remote_copy(
            src_ref=v_ref.at[which, pl.ds(half * RHS, RHS), pl.ds(start, PIECE)],
            dst_ref=p_ref.at[which, me],
            send_sem=part_send.at[which, half, block],
            recv_sem=part_recv.at[which],
            device_id=(half, area * 2 + block // 4, block % 4),
            device_id_type=MESH,
        )

    def part_store(which, block, total):
        start = pl.multiple_of(block * PIECE, PIECE)
        v_ref[which, :, pl.ds(start, PIECE)] = total
        for half in range(2):

            @pl.when(jnp.logical_or(block != mine, mirror != half))
            def _():
                part_copy(which, half, block).start()

        @pl.when(jnp.logical_and(block == mine, mirror == 0))
        def _():
            p_ref[which, me] = total[0:RHS]

        @pl.when(jnp.logical_and(block == mine, mirror == 1))
        def _():
            p_ref[which, me] = total[RHS : 2 * RHS]

    def part_sum(which):
        others = p_ref.at[which, 0 : SENDERS - 1]
        pltpu.make_async_copy(others, others, part_recv.at[which]).wait()
        total = p_ref[which, 0]
        for k in range(1, SENDERS):
            total += p_ref[which, k]
        return total

    store_terms(gs_ref, fs_ref, True)
    store_terms(gt_ref, ft_ref, False)
    r_ref[...] = ft_ref[...].astype(BF16)
    zt_ref[0:1, :] = (gt_ref[2:3, :] - 2.0) * ROOT
    zt_ref[1:2, :] = gt_ref[1:2, :]
    l_ref[...] = jnp.transpose(fs_ref[...]).astype(BF16)
    term = lax.broadcasted_iota(jnp.int32, (TERMS, 128), 0)
    pick_z = ((term >= 18) & (term < 21)).astype(BF16)
    pick_y = ((term == 6) | (term == 10) | (term == 11)).astype(BF16)

    def spread(i, carry):
        at = pl.ds(pl.multiple_of(i * 512, 512), 512)
        left = l_ref[at, :]
        zb_ref[at, :] = jnp.dot(left, pick_z, preferred_element_type=F32) * ROOT
        yb_ref[at, :] = (jnp.dot(left, pick_y, preferred_element_type=F32) + 0.25) * (4.0 * SQUARE)
        return carry

    lax.fori_loop(0, SOURCES // 512, spread, 0)

    def make_tile(at, block):
        start = pl.multiple_of(block * PIECE, PIECE)
        rest = jnp.dot(l_ref[at, :], r_ref[:, pl.ds(start, PIECE)], preferred_element_type=F32)
        zb, yb = zb_ref[at, :], yb_ref[at, :]
        near, far = [], []
        for c in range(PIECE // 128):
            lanes = pl.ds(start + c * 128, 128)
            dz = zb - zt_ref[0:1, lanes]
            squared = dz * dz + rest[:, c * 128 : (c + 1) * 128]
            near.append(lax.rsqrt(squared).astype(BF16))
            far.append(lax.rsqrt(squared + yb * zt_ref[1:2, lanes]).astype(BF16))
        near, far = jnp.concatenate(near, 1), jnp.concatenate(far, 1)
        a_ref[at, pl.ds(start, PIECE)] = near
        b_ref[at, pl.ds(start, PIECE)] = far
        return near, far

    def swap(value):
        return jnp.concatenate([value[RHS:], value[:RHS]], 0)

    def build(block):
        def step(i, carry):
            make_tile(pl.ds(pl.multiple_of(i * CHUNK, CHUNK), CHUNK), block)
            return carry

        lax.fori_loop(0, SOURCES // CHUNK, step, 0, unroll=8)

    def build_and_apply(block):
        def step(i, total):
            at = pl.ds(pl.multiple_of(i * CHUNK, CHUNK), CHUNK)
            near, far = make_tile(at, block)
            part = j_ref[0, :, at]
            total += jnp.dot(part, near, preferred_element_type=F32)
            return total + swap(jnp.dot(part, far, preferred_element_type=F32))

        zero = jnp.zeros((2 * RHS, PIECE), F32)
        return lax.fori_loop(0, SOURCES // CHUNK, step, zero, unroll=SOURCES // CHUNK)

    def apply(which, block):
        at = pl.ds(pl.multiple_of(block * PIECE, PIECE), PIECE)
        part = j_ref[which]
        return jnp.dot(part, a_ref[:, at], preferred_element_type=F32) + swap(
            jnp.dot(part, b_ref[:, at], preferred_element_type=F32)
        )

    pl.semaphore_wait(barrier, jnp.where(home == mirror, 31, 32) + SENDERS - 1)
    gather_start(0)
    build(mine)
    gather_wait(0)

    def first(i, carry):
        block = (mine + 1 + i) % BLOCKS
        part_store(0, block, build_and_apply(block))
        return carry

    lax.fori_loop(0, BLOCKS - 1, first, 0)
    part_store(0, mine, apply(0, mine))
    residual = right_ref[...] - part_sum(0)
    res_ref[...] = residual
    own_ref[1] = residual.astype(BF16)

    gather_start(1)
    gather_wait(1)

    def second(i, carry):
        block = (mine + 1 + i) % BLOCKS
        part_store(1, block, apply(1, block))
        return carry

    lax.fori_loop(0, BLOCKS, second, 0)
    img_ref[...] = part_sum(1)

    for which in range(2):

        def gathered(j, carry):
            @pl.when(jnp.logical_not(is_self(j)))
            def _():
                gather_copy(which, j).wait_send()

            return carry

        lax.fori_loop(0, 32, gathered, 0)

        def parted(block, carry):
            for half in range(2):

                @pl.when(jnp.logical_or(block != mine, mirror != half))
                def _():
                    part_copy(which, half, block).wait_send()

            return carry

        lax.fori_loop(0, BLOCKS, parted, 0)


def on_device(currents, right_side, geometry):
    vmem = pl.BlockSpec(memory_space=pltpu.VMEM)
    owned = jax.ShapeDtypeStruct((RHS, PIECE), F32)
    return pl.pallas_call(
        kernel,
        out_shape=(owned, owned),
        in_specs=[vmem, vmem, pl.BlockSpec(memory_space=pl.ANY)],
        out_specs=(vmem, vmem),
        scratch_shapes=[
            pltpu.VMEM((SOURCES, TARGETS), BF16),
            pltpu.VMEM((SOURCES, TARGETS), BF16),
            pltpu.VMEM((4, SOURCES), F32),
            pltpu.VMEM((4, TARGETS), F32),
            pltpu.VMEM((TERMS, SOURCES), F32),
            pltpu.VMEM((TERMS, TARGETS), F32),
            pltpu.VMEM((SOURCES, TERMS), BF16),
            pltpu.VMEM((TERMS, TARGETS), BF16),
            pltpu.VMEM((SOURCES, 128), F32),
            pltpu.VMEM((SOURCES, 128), F32),
            pltpu.VMEM((2, TARGETS), F32),
            pltpu.VMEM((2, RHS, PIECE), BF16),
            pltpu.VMEM((2, 2 * RHS, SOURCES), BF16),
            pltpu.VMEM((2, 2 * RHS, TARGETS), F32),
            pltpu.VMEM((2, SENDERS, RHS, PIECE), F32),
            pltpu.SemaphoreType.DMA((2,)),
            pltpu.SemaphoreType.DMA((2, 32)),
            pltpu.SemaphoreType.DMA((2,)),
            pltpu.SemaphoreType.DMA((2, 2, BLOCKS)),
            pltpu.SemaphoreType.DMA((2,)),
        ],
        compiler_params=pltpu.CompilerParams(
            collective_id=0, has_side_effects=True, vmem_limit_bytes=58 * 1024 * 1024
        ),
        name="peec_pair_products",
    )(currents, right_side, geometry)


def solution(mesh):
    placed = (P(None, ("mirror", "rows")), P(None, ("mirror", "rows", "cols")), P())
    return jax.shard_map(
        on_device,
        mesh=mesh,
        in_specs=placed,
        out_specs=(P(None, ("mirror", "rows", "cols")), P(None, ("mirror", "rows", "cols"))),
        check_vma=False,
    )
```

time: 1220 us -> 77.9 us (0.06)
  the two profiles are of different devices: /device:TPU:255 before, /device:TPU:1 now
where the time goes in v1:
time: 77.9 us; the launch traced here: 77.2 us
  Pallas kernels  74.6 us (96%)
  local copies, waits for them, and re-layouts  1.94 us (2%)
    pallas_call x1, Pallas kernels, on_device(): pl.pallas_call(kernel, out_shape=(owned, owned), in_specs=[vmem, vmem, pl...  74.6 us
    unnamed x4, local copies, waits for them, and re-layouts  1.94 us

profile of v1, /device:TPU:1, one launch (start us, length us, event | category | flops | bytes accessed | tf_op | source)
XLA Modules:
  0.0 77.2 jit_solution(13233785851189697576)
XLA Ops:
  0.6 74.6 %peec_pair_products.1 = (f32[16,256]{1,0:T(8,128)}, f32[16,256]{1,0:T(8,128)}) custom-call(bf16[16,1024]{1,0:T(8,128)(2,1)} %cur_ref.1, f32[16,256]{1,0:T(8,128)} %right_ref.1, f32[4,65536]{1,0:T(4,128)} %geo_ref.1), custom_call_target="tpu_custom_call" | custom-call | tf_op jit(solution)/shard_map/peec_pair_products/pallas_call | solution.py:298
  75.2 0.0 copy-start
  75.2 1.3 %copy.7 = f32[16,256]{1,0:T(8,128)} copy(f32[16,256]{1,0:T(8,128)} %get-tuple-element.4) | data formatting | bytes 32768
  76.6 0.0 copy-done
  76.6 0.6 copy.8
Async XLA Ops:
  75.2 1.3 %copy-start = (f32[16,256]{1,0:T(8,128)S(1)}, f32[16,256]{1,0:T(8,128)}, u32[]{:S(2)}) copy-start(f32[16,256]{1,0:T(8,128)} %get-tuple-element.5) | copy-start | bytes 49156

commit v2 on v1

--- a/solution.py
+++ b/solution.py
@@ -52,96 +52,118 @@
     cur_ref, right_ref, geo_ref, res_ref, img_ref,
     a_ref, b_ref, gs_ref, gt_ref, fs_ref, ft_ref, l_ref, r_ref, zb_ref, yb_ref, zt_ref,
     own_ref, j_ref, v_ref, p_ref,
-    geo_sem, gather_send, gather_recv, part_send, part_recv,
+    geo_sem, gather_send, gather_recv, core_send, core_recv, part_send, part_recv,
 ):
     mirror = lax.axis_index("mirror")
     row = lax.axis_index("rows")
     col = lax.axis_index("cols")
     core = row % 2
-    home = row // 32
-    slot = (row % 32) // 2
-    area = row // 2
-    me = mirror * 8 + core * 4 + col
-    mine = core * 4 + col
+    depth = row // 8
+    line = (row // 2) % 4
+    home = col // 2
+    slot = core * 8 + line * 2 + col % 2
+    me = mirror * 8 + depth
 
     barrier = pltpu.get_barrier_semaphore()
 
+    def greet(other):
+        pl.semaphore_signal(barrier, inc=1, device_id=other, device_id_type=MESH)
+
     def greet_source(k, carry):
-        for half in range(2):
-            other = mirror * 32 + 2 * k + core
-
-            @pl.when(jnp.logical_or(other != row, mirror != half))
-            def _():
-                pl.semaphore_signal(barrier, inc=1, device_id=(half, other, col), device_id_type=MESH)
-
-        return carry
-
-    lax.fori_loop(0, PIECES, greet_source, 0)
+        other = (k // 8, depth * 8 + (k // 2) % 4 * 2 + core, mirror * 2 + k % 2)
+
+        @pl.when(jnp.logical_not(is_self(*other)))
+        def _():
+            greet(other)
+
+        return carry
+
+    def is_self(half, other, column):
+        return jnp.logical_and(jnp.logical_and(half == mirror, other == row), column == col)
 
     def greet_part(k, carry):
         @pl.when(k != me)
         def _():
-            pl.semaphore_signal(
-                barrier, inc=1, device_id=(k // 8, area * 2 + (k // 4) % 2, k % 4), device_id_type=MESH
-            )
-
-        return carry
-
+            greet((k // 8, k % 8 * 8 + line * 2 + core, col))
+
+        return carry
+
+    sibling = (mirror, row + 1 - 2 * core, col)
+    lax.fori_loop(0, 16, greet_source, 0)
     lax.fori_loop(0, SENDERS, greet_part, 0)
+    greet(sibling)
 
     def source_geo(k, carry):
-        start = pl.multiple_of((mirror * 32 + 2 * k + core) * 1024 + col * PIECE, PIECE)
-        into = pl.multiple_of(k * PIECE, PIECE)
+        start = (depth * 8 + (k // 2) % 4 * 2 + k // 8) * 1024 + (mirror * 2 + k % 2) * PIECE
         pltpu.make_async_copy(
-            geo_ref.at[:, pl.ds(start, PIECE)], gs_ref.at[:, pl.ds(into, PIECE)], geo_sem.at[0]
+            geo_ref.at[:, pl.ds(pl.multiple_of(start, PIECE), PIECE)],
+            gs_ref.at[:, pl.ds(pl.multiple_of(k * PIECE, PIECE), PIECE)],
+            geo_sem.at[0],
         ).start()
         return carry
 
+    def target_geo(k, carry):
+        start = (k * 8 + line * 2 + core) * 1024 + col * PIECE
+        pltpu.make_async_copy(
+            geo_ref.at[:, pl.ds(pl.multiple_of(start, PIECE), PIECE)],
+            gt_ref.at[:, pl.ds(pl.multiple_of(k * PIECE, PIECE), PIECE)],
+            geo_sem.at[1],
+        ).start()
+        return carry
+
     lax.fori_loop(0, PIECES, source_geo, 0)
-    first = pl.multiple_of(area * TARGETS, TARGETS)
-    target_geo = pltpu.make_async_copy(geo_ref.at[:, pl.ds(first, TARGETS)], gt_ref, geo_sem.at[1])
-    target_geo.start()
+    lax.fori_loop(0, BLOCKS, target_geo, 0)
     own_ref[0] = cur_ref[:, pl.ds(pl.multiple_of(col * PIECE, PIECE), PIECE)]
-    pltpu.make_async_copy(geo_ref.at[:, pl.ds(0, SOURCES)], gs_ref, geo_sem.at[0]).wait()
-    target_geo.wait()
-
-    def gather_copy(which, j):
-        into = pl.multiple_of(slot * PIECE, PIECE)
+
+    def piece_at(which):
+        rows = pl.ds(pl.multiple_of(mirror * RHS, RHS), RHS)
+        return j_ref.at[which, rows, pl.ds(pl.multiple_of(slot * PIECE, PIECE), PIECE)]
+
+    def gather_copy(which, i):
         return pltpu.make_async_remote_copy(
             src_ref=own_ref.at[which],
-            dst_ref=j_ref.at[which, pl.ds(pl.multiple_of(mirror * RHS, RHS), RHS), pl.ds(into, PIECE)],
-            send_sem=gather_send.at[which, j],
+            dst_ref=piece_at(which),
+            send_sem=gather_send.at[which, i],
             recv_sem=gather_recv.at[which],
-            device_id=(home, 2 * j + core, col),
+            device_id=taker(i),
             device_id_type=MESH,
         )
 
-    def is_self(j):
-        return jnp.logical_and(home == mirror, 2 * j + core == row)
+    def taker(i):
+        return home, depth * 8 + (line + i // 4) % 4 * 2 + core, (col + i) % 4
 
     def gather_start(which):
         def send(i, carry):
-            j = (area + i) % 32
-
-            @pl.when(jnp.logical_not(is_self(j)))
+            @pl.when(jnp.logical_not(is_self(*taker(i))))
             def _():
-                gather_copy(which, j).start()
-
-            @pl.when(is_self(j))
-            def _():
-                into = pl.multiple_of(slot * PIECE, PIECE)
-                pltpu.make_async_copy(
-                    own_ref.at[which],
-                    j_ref.at[which, pl.ds(pl.multiple_of(mirror * RHS, RHS), RHS), pl.ds(into, PIECE)],
-                    gather_recv.at[which],
-                ).start()
+                gather_copy(which, i).start()
 
             return carry
 
-        lax.fori_loop(0, 32, send, 0)
+        lax.fori_loop(0, 16, send, 0)
+
+        @pl.when(home == mirror)
+        def _():
+            pltpu.make_async_copy(own_ref.at[which], piece_at(which), gather_recv.at[which]).start()
+
+    def core_part(which, side):
+        return j_ref.at[which, :, pl.ds(pl.multiple_of(side * (SOURCES // 2), SOURCES // 2), SOURCES // 2)]
+
+    def core_copy(which):
+        return pltpu.make_async_remote_copy(
+            src_ref=core_part(which, core),
+            dst_ref=core_part(which, core),
+            send_sem=core_send.at[which],
+            recv_sem=core_recv.at[which],
+            device_id=sibling,
+            device_id_type=MESH,
+        )
 
     def gather_wait(which):
-        pltpu.make_async_copy(j_ref.at[which], j_ref.at[which], gather_recv.at[which]).wait()
+        mine = core_part(which, core)
+        pltpu.make_async_copy(mine, mine, gather_recv.at[which]).wait()
+        core_copy(which).start()
+        core_copy(which).wait_recv()
 
     def part_copy(which, half, block):
         start = pl.multiple_of(block * PIECE, PIECE)
@@ -150,7 +172,7 @@
             dst_ref=p_ref.at[which, me],
             send_sem=part_send.at[which, half, block],
             recv_sem=part_recv.at[which],
-            device_id=(half, area * 2 + block // 4, block % 4),
+            device_id=(half, block * 8 + line * 2 + core, col),
             device_id_type=MESH,
         )
 
@@ -159,15 +181,15 @@
         v_ref[which, :, pl.ds(start, PIECE)] = total
         for half in range(2):
 
-            @pl.when(jnp.logical_or(block != mine, mirror != half))
+            @pl.when(jnp.logical_or(block != depth, mirror != half))
             def _():
                 part_copy(which, half, block).start()
 
-        @pl.when(jnp.logical_and(block == mine, mirror == 0))
+        @pl.when(jnp.logical_and(block == depth, mirror == 0))
         def _():
             p_ref[which, me] = total[0:RHS]
 
-        @pl.when(jnp.logical_and(block == mine, mirror == 1))
+        @pl.when(jnp.logical_and(block == depth, mirror == 1))
         def _():
             p_ref[which, me] = total[RHS : 2 * RHS]
 
@@ -179,6 +201,11 @@
             total += p_ref[which, k]
         return total
 
+    pl.semaphore_wait(barrier, jnp.where(home == mirror, 15, 16) + SENDERS)
+    gather_start(0)
+
+    pltpu.make_async_copy(gs_ref, gs_ref, geo_sem.at[0]).wait()
+    pltpu.make_async_copy(gt_ref, gt_ref, geo_sem.at[1]).wait()
     store_terms(gs_ref, fs_ref, True)
     store_terms(gt_ref, ft_ref, False)
     r_ref[...] = ft_ref[...].astype(BF16)
@@ -242,18 +269,16 @@
             jnp.dot(part, b_ref[:, at], preferred_element_type=F32)
         )
 
-    pl.semaphore_wait(barrier, jnp.where(home == mirror, 31, 32) + SENDERS - 1)
-    gather_start(0)
-    build(mine)
+    build(depth)
     gather_wait(0)
 
     def first(i, carry):
-        block = (mine + 1 + i) % BLOCKS
+        block = (depth + 1 + i) % BLOCKS
         part_store(0, block, build_and_apply(block))
         return carry
 
     lax.fori_loop(0, BLOCKS - 1, first, 0)
-    part_store(0, mine, apply(0, mine))
+    part_store(0, depth, apply(0, depth))
     residual = right_ref[...] - part_sum(0)
     res_ref[...] = residual
     own_ref[1] = residual.astype(BF16)
@@ -262,7 +287,7 @@
     gather_wait(1)
 
     def second(i, carry):
-        block = (mine + 1 + i) % BLOCKS
+        block = (depth + 1 + i) % BLOCKS
         part_store(1, block, apply(1, block))
         return carry
 
@@ -271,19 +296,21 @@
 
     for which in range(2):
 
-        def gathered(j, carry):
-            @pl.when(jnp.logical_not(is_self(j)))
+        core_copy(which).wait_send()
+
+        def gathered(i, carry):
+            @pl.when(jnp.logical_not(is_self(*taker(i))))
             def _():
-                gather_copy(which, j).wait_send()
+                gather_copy(which, i).wait_send()
 
             return carry
 
-        lax.fori_loop(0, 32, gathered, 0)
+        lax.fori_loop(0, 16, gathered, 0)
 
         def parted(block, carry):
             for half in range(2):
 
-                @pl.when(jnp.logical_or(block != mine, mirror != half))
+                @pl.when(jnp.logical_or(block != depth, mirror != half))
                 def _():
                     part_copy(which, half, block).wait_send()
 
@@ -317,7 +344,9 @@
             pltpu.VMEM((2, 2 * RHS, TARGETS), F32),
             pltpu.VMEM((2, SENDERS, RHS, PIECE), F32),
             pltpu.SemaphoreType.DMA((2,)),
-            pltpu.SemaphoreType.DMA((2, 32)),
+            pltpu.SemaphoreType.DMA((2, 16)),
+            pltpu.SemaphoreType.DMA((2,)),
+            pltpu.SemaphoreType.DMA((2,)),
             pltpu.SemaphoreType.DMA((2,)),
             pltpu.SemaphoreType.DMA((2, 2, BLOCKS)),
             pltpu.SemaphoreType.DMA((2,)),

time: 77.9 us -> 69.4 us (0.89)
  Pallas kernels: 74.6 us -> 66.2 us
    pallas_call x1, Pallas kernels: 74.6 us -> 66.2 us  [on_device(): pl.pallas_call(kernel, out_shape=(owned, owned), in_specs=[vmem, vmem, pl...]
where the time goes in v2:
time: 69.4 us; the launch traced here: 68.8 us
  Pallas kernels  66.2 us (95%)
  local copies, waits for them, and re-layouts  1.94 us (3%)
    pallas_call x1, Pallas kernels, on_device(): pl.pallas_call(kernel, out_shape=(owned, owned), in_specs=[vmem, vmem, pl...  66.2 us
    unnamed x4, local copies, waits for them, and re-layouts  1.94 us

profile of v2, /device:TPU:1, one launch (start us, length us, event | category | flops | bytes accessed | tf_op | source)
XLA Modules:
  0.0 68.8 jit_solution(9430734230826633426)
XLA Ops:
  0.6 66.2 %peec_pair_products.1 = (f32[16,256]{1,0:T(8,128)}, f32[16,256]{1,0:T(8,128)}) custom-call(bf16[16,1024]{1,0:T(8,128)(2,1)} %cur_ref.1, f32[16,256]{1,0:T(8,128)} %right_ref.1, f32[4,65536]{1,0:T(4,128)} %geo_ref.1), custom_call_target="tpu_custom_call" | custom-call | tf_op jit(solution)/shard_map/peec_pair_products/pallas_call | solution.py:325
  66.8 0.0 copy-start
  66.8 1.3 %copy.7 = f32[16,256]{1,0:T(8,128)} copy(f32[16,256]{1,0:T(8,128)} %get-tuple-element.4) | data formatting | bytes 32768
  68.2 0.0 copy-done
  68.2 0.6 copy.8
Async XLA Ops:
  66.8 1.3 %copy-start = (f32[16,256]{1,0:T(8,128)S(1)}, f32[16,256]{1,0:T(8,128)}, u32[]{:S(2)}) copy-start(f32[16,256]{1,0:T(8,128)} %get-tuple-element.5) | copy-start | bytes 49156

commit v3 on v2

--- a/solution.py
+++ b/solution.py
@@ -21,6 +21,7 @@
 ROOT = 2.0**8.5
 CHUNK = 256
 SENDERS = 16
+FUSED = 3
 
 
 def split3(value):
@@ -60,6 +61,7 @@
     core = row % 2
     depth = row // 8
     line = (row // 2) % 4
+    across = (line + 2) % 4
     home = col // 2
     slot = core * 8 + line * 2 + col % 2
     me = mirror * 8 + depth
@@ -82,10 +84,7 @@
         return jnp.logical_and(jnp.logical_and(half == mirror, other == row), column == col)
 
     def greet_part(k, carry):
-        @pl.when(k != me)
-        def _():
-            greet((k // 8, k % 8 * 8 + line * 2 + core, col))
-
+        greet((k // 8, k % 8 * 8 + across * 2 + core, col))
         return carry
 
     sibling = (mirror, row + 1 - 2 * core, col)
@@ -103,7 +102,7 @@
         return carry
 
     def target_geo(k, carry):
-        start = (k * 8 + line * 2 + core) * 1024 + col * PIECE
+        start = (k * 8 + across * 2 + core) * 1024 + col * PIECE
         pltpu.make_async_copy(
             geo_ref.at[:, pl.ds(pl.multiple_of(start, PIECE), PIECE)],
             gt_ref.at[:, pl.ds(pl.multiple_of(k * PIECE, PIECE), PIECE)],
@@ -172,7 +171,7 @@
             dst_ref=p_ref.at[which, me],
             send_sem=part_send.at[which, half, block],
             recv_sem=part_recv.at[which],
-            device_id=(half, block * 8 + line * 2 + core, col),
+            device_id=(half, block * 8 + across * 2 + core, col),
             device_id_type=MESH,
         )
 
@@ -180,28 +179,16 @@
         start = pl.multiple_of(block * PIECE, PIECE)
         v_ref[which, :, pl.ds(start, PIECE)] = total
         for half in range(2):
-
-            @pl.when(jnp.logical_or(block != depth, mirror != half))
-            def _():
-                part_copy(which, half, block).start()
-
-        @pl.when(jnp.logical_and(block == depth, mirror == 0))
-        def _():
-            p_ref[which, me] = total[0:RHS]
-
-        @pl.when(jnp.logical_and(block == depth, mirror == 1))
-        def _():
-            p_ref[which, me] = total[RHS : 2 * RHS]
+            part_copy(which, half, block).start()
 
     def part_sum(which):
-        others = p_ref.at[which, 0 : SENDERS - 1]
-        pltpu.make_async_copy(others, others, part_recv.at[which]).wait()
+        pltpu.make_async_copy(p_ref.at[which], p_ref.at[which], part_recv.at[which]).wait()
         total = p_ref[which, 0]
         for k in range(1, SENDERS):
             total += p_ref[which, k]
         return total
 
-    pl.semaphore_wait(barrier, jnp.where(home == mirror, 15, 16) + SENDERS)
+    pl.semaphore_wait(barrier, jnp.where(home == mirror, 15, 16) + SENDERS + 1)
     gather_start(0)
 
     pltpu.make_async_copy(gs_ref, gs_ref, geo_sem.at[0]).wait()
@@ -249,7 +236,7 @@
             make_tile(pl.ds(pl.multiple_of(i * CHUNK, CHUNK), CHUNK), block)
             return carry
 
-        lax.fori_loop(0, SOURCES // CHUNK, step, 0, unroll=8)
+        lax.fori_loop(0, SOURCES // CHUNK, step, 0, unroll=SOURCES // CHUNK)
 
     def build_and_apply(block):
         def step(i, total):
@@ -269,16 +256,30 @@
             jnp.dot(part, b_ref[:, at], preferred_element_type=F32)
         )
 
-    build(depth)
+    def block_of(i):
+        reach = (i + 1) // 2
+        return (depth + 4 + reach * (2 * ((i + 1) % 2) - 1)) % BLOCKS
+
+    def ahead(i, carry):
+        build(block_of(i))
+        return carry
+
+    lax.fori_loop(FUSED, BLOCKS, ahead, 0)
     gather_wait(0)
 
     def first(i, carry):
-        block = (depth + 1 + i) % BLOCKS
+        block = block_of(i)
         part_store(0, block, build_and_apply(block))
         return carry
 
-    lax.fori_loop(0, BLOCKS - 1, first, 0)
-    part_store(0, depth, apply(0, depth))
+    lax.fori_loop(0, FUSED, first, 0)
+
+    def rest(i, carry):
+        block = block_of(i)
+        part_store(0, block, apply(0, block))
+        return carry
+
+    lax.fori_loop(FUSED, BLOCKS, rest, 0)
     residual = right_ref[...] - part_sum(0)
     res_ref[...] = residual
     own_ref[1] = residual.astype(BF16)
@@ -287,7 +288,7 @@
     gather_wait(1)
 
     def second(i, carry):
-        block = (depth + 1 + i) % BLOCKS
+        block = block_of(i)
         part_store(1, block, apply(1, block))
         return carry
 
@@ -309,10 +310,7 @@
 
         def parted(block, carry):
             for half in range(2):
-
-                @pl.when(jnp.logical_or(block != depth, mirror != half))
-                def _():
-                    part_copy(which, half, block).wait_send()
+                part_copy(which, half, block).wait_send()
 
             return carry
 

time: 69.4 us -> 65.4 us (0.942)
  Pallas kernels: 66.2 us -> 62.5 us
    pallas_call x1, Pallas kernels: 66.2 us -> 62.5 us  [on_device(): pl.pallas_call(kernel, out_shape=(owned, owned), in_specs=[vmem, vmem, pl...]
where the time goes in v3:
time: 65.4 us; the launch traced here: 65.1 us
  Pallas kernels  62.5 us (96%)
  local copies, waits for them, and re-layouts  1.94 us (3%)
    pallas_call x1, Pallas kernels, on_device(): pl.pallas_call(kernel, out_shape=(owned, owned), in_specs=[vmem, vmem, pl...  62.5 us
    unnamed x4, local copies, waits for them, and re-layouts  1.94 us

profile of v3, /device:TPU:1, one launch (start us, length us, event | category | flops | bytes accessed | tf_op | source)
XLA Modules:
  0.0 65.1 jit_solution(14867259430621425549)
XLA Ops:
  0.6 62.5 %peec_pair_products.1 = (f32[16,256]{1,0:T(8,128)}, f32[16,256]{1,0:T(8,128)}) custom-call(bf16[16,1024]{1,0:T(8,128)(2,1)} %cur_ref.1, f32[16,256]{1,0:T(8,128)} %right_ref.1, f32[4,65536]{1,0:T(4,128)} %geo_ref.1), custom_call_target="tpu_custom_call" | custom-call | tf_op jit(solution)/shard_map/peec_pair_products/pallas_call | solution.py:323
  63.2 0.0 copy-start
  63.2 1.3 %copy.7 = f32[16,256]{1,0:T(8,128)} copy(f32[16,256]{1,0:T(8,128)} %get-tuple-element.4) | data formatting | bytes 32768
  64.5 0.0 copy-done
  64.5 0.6 copy.8
Async XLA Ops:
  63.2 1.3 %copy-start = (f32[16,256]{1,0:T(8,128)S(1)}, f32[16,256]{1,0:T(8,128)}, u32[]{:S(2)}) copy-start(f32[16,256]{1,0:T(8,128)} %get-tuple-element.5) | copy-start | bytes 49156

commit v4 on v3

--- a/solution.py
+++ b/solution.py
@@ -15,12 +15,14 @@
 SOURCES = 4096
 TARGETS = 2048
 PIECES = SOURCES // PIECE
+PART = 2 * PIECE
 BLOCKS = TARGETS // PIECE
 TERMS = 32
 SQUARE = 2.0**17
 ROOT = 2.0**8.5
 CHUNK = 256
 SENDERS = 16
+NEAREST = (2, 1, 3, 0)
 FUSED = 3
 
 
@@ -62,6 +64,7 @@
     depth = row // 8
     line = (row // 2) % 4
     across = (line + 2) % 4
+    own_set = (mirror + line) % 2
     home = col // 2
     slot = core * 8 + line * 2 + col % 2
     me = mirror * 8 + depth
@@ -72,7 +75,7 @@
         pl.semaphore_signal(barrier, inc=1, device_id=other, device_id_type=MESH)
 
     def greet_source(k, carry):
-        other = (k // 8, depth * 8 + (k // 2) % 4 * 2 + core, mirror * 2 + k % 2)
+        other = (k // 8, depth * 8 + (k // 2) % 4 * 2 + core, own_set * 2 + k % 2)
 
         @pl.when(jnp.logical_not(is_self(*other)))
         def _():
@@ -93,7 +96,7 @@
     greet(sibling)
 
     def source_geo(k, carry):
-        start = (depth * 8 + (k // 2) % 4 * 2 + k // 8) * 1024 + (mirror * 2 + k % 2) * PIECE
+        start = (depth * 8 + (k // 2) % 4 * 2 + k // 8) * 1024 + (own_set * 2 + k % 2) * PIECE
         pltpu.make_async_copy(
             geo_ref.at[:, pl.ds(pl.multiple_of(start, PIECE), PIECE)],
             gs_ref.at[:, pl.ds(pl.multiple_of(k * PIECE, PIECE), PIECE)],
@@ -123,13 +126,14 @@
             src_ref=own_ref.at[which],
             dst_ref=piece_at(which),
             send_sem=gather_send.at[which, i],
-            recv_sem=gather_recv.at[which],
+            recv_sem=gather_recv.at[which, line],
             device_id=taker(i),
             device_id_type=MESH,
         )
 
     def taker(i):
-        return home, depth * 8 + (line + i // 4) % 4 * 2 + core, (col + i) % 4
+        other = (line + 2 + i // 4) % 4
+        return (home + other) % 2, depth * 8 + other * 2 + core, (col + i) % 4
 
     def gather_start(which):
         def send(i, carry):
@@ -141,28 +145,33 @@
 
         lax.fori_loop(0, 16, send, 0)
 
-        @pl.when(home == mirror)
+        @pl.when(home == own_set)
         def _():
-            pltpu.make_async_copy(own_ref.at[which], piece_at(which), gather_recv.at[which]).start()
-
-    def core_part(which, side):
-        return j_ref.at[which, :, pl.ds(pl.multiple_of(side * (SOURCES // 2), SOURCES // 2), SOURCES // 2)]
-
-    def core_copy(which):
+            pltpu.make_async_copy(own_ref.at[which], piece_at(which), gather_recv.at[which, line]).start()
+
+    def chunk_at(side, away):
+        start = side * (SOURCES // 2) + (line + away) % 4 * PART
+        return pl.ds(pl.multiple_of(start, PART), PART)
+
+    def core_copy(which, away):
+        part = j_ref.at[which, :, chunk_at(core, away)]
         return pltpu.make_async_remote_copy(
-            src_ref=core_part(which, core),
-            dst_ref=core_part(which, core),
-            send_sem=core_send.at[which],
-            recv_sem=core_recv.at[which],
+            src_ref=part,
+            dst_ref=part,
+            send_sem=core_send.at[which, (line + away) % 4],
+            recv_sem=core_recv.at[which, (line + away) % 4],
             device_id=sibling,
             device_id_type=MESH,
         )
 
-    def gather_wait(which):
-        mine = core_part(which, core)
-        pltpu.make_async_copy(mine, mine, gather_recv.at[which]).wait()
-        core_copy(which).start()
-        core_copy(which).wait_recv()
+    def take(which, away):
+        part = j_ref.at[which, :, chunk_at(core, away)]
+        pltpu.make_async_copy(part, part, gather_recv.at[which, (line + away) % 4]).wait()
+        core_copy(which, away).start()
+
+    def take_other(which, away):
+        part = j_ref.at[which, :, chunk_at(1 - core, away)]
+        pltpu.make_async_copy(part, part, core_recv.at[which, (line + away) % 4]).wait()
 
     def part_copy(which, half, block):
         start = pl.multiple_of(block * PIECE, PIECE)
@@ -188,7 +197,7 @@
             total += p_ref[which, k]
         return total
 
-    pl.semaphore_wait(barrier, jnp.where(home == mirror, 15, 16) + SENDERS + 1)
+    pl.semaphore_wait(barrier, jnp.where(home == own_set, 15, 16) + SENDERS + 1)
     gather_start(0)
 
     pltpu.make_async_copy(gs_ref, gs_ref, geo_sem.at[0]).wait()
@@ -260,12 +269,19 @@
         reach = (i + 1) // 2
         return (depth + 4 + reach * (2 * ((i + 1) % 2) - 1)) % BLOCKS
 
-    def ahead(i, carry):
+    def hand_over(i, carry):
         build(block_of(i))
-        return carry
-
-    lax.fori_loop(FUSED, BLOCKS, ahead, 0)
-    gather_wait(0)
+
+        @pl.when(i == BLOCKS - 2)
+        def _():
+            for away in NEAREST:
+                take(0, away)
+
+        return carry
+
+    lax.fori_loop(FUSED, BLOCKS, hand_over, 0)
+    for away in NEAREST:
+        take_other(0, away)
 
     def first(i, carry):
         block = block_of(i)
@@ -285,11 +301,41 @@
     own_ref[1] = residual.astype(BF16)
 
     gather_start(1)
-    gather_wait(1)
+
+    def product(chunk, columns):
+        part = j_ref[1, :, chunk]
+        return jnp.dot(part, a_ref[chunk, columns], preferred_element_type=F32) + swap(
+            jnp.dot(part, b_ref[chunk, columns], preferred_element_type=F32)
+        )
+
+    def sum_chunk(chunk, fresh):
+        def step(i, carry):
+            columns = pl.ds(pl.multiple_of(i * PART, PART), PART)
+            total = product(chunk, columns)
+            v_ref[1, :, columns] = total if fresh else v_ref[1, :, columns] + total
+            return carry
+
+        lax.fori_loop(0, TARGETS // PART, step, 0)
+
+    take(1, 2)
+    sum_chunk(chunk_at(core, 2), True)
+    take(1, 1)
+    sum_chunk(chunk_at(core, 1), False)
+    take_other(1, 2)
+    sum_chunk(chunk_at(1 - core, 2), False)
+    take(1, 3)
+    sum_chunk(chunk_at(core, 3), False)
+    take(1, 0)
+    for away in (1, 3, 0):
+        take_other(1, away)
 
     def second(i, carry):
         block = block_of(i)
-        part_store(1, block, apply(1, block))
+        columns = pl.ds(pl.multiple_of(block * PIECE, PIECE), PIECE)
+        total = v_ref[1, :, columns] + product(chunk_at(core, 0), columns)
+        for away in (1, 3, 0):
+            total += product(chunk_at(1 - core, away), columns)
+        part_store(1, block, total)
         return carry
 
     lax.fori_loop(0, BLOCKS, second, 0)
@@ -297,7 +343,8 @@
 
     for which in range(2):
 
-        core_copy(which).wait_send()
+        for away in NEAREST:
+            core_copy(which, away).wait_send()
 
         def gathered(i, carry):
             @pl.when(jnp.logical_not(is_self(*taker(i))))
@@ -317,10 +364,21 @@
         lax.fori_loop(0, BLOCKS, parted, 0)
 
 
+def settle(residual, image, residual_out, image_out, sems):
+    copies = [
+        pltpu.make_async_copy(residual, residual_out, sems.at[0]),
+        pltpu.make_async_copy(image, image_out, sems.at[1]),
+    ]
+    for copy in copies:
+        copy.start()
+    for copy in copies:
+        copy.wait()
+
+
 def on_device(currents, right_side, geometry):
     vmem = pl.BlockSpec(memory_space=pltpu.VMEM)
     owned = jax.ShapeDtypeStruct((RHS, PIECE), F32)
-    return pl.pallas_call(
+    residual, image = pl.pallas_call(
         kernel,
         out_shape=(owned, owned),
         in_specs=[vmem, vmem, pl.BlockSpec(memory_space=pl.ANY)],
@@ -343,9 +401,9 @@
             pltpu.VMEM((2, SENDERS, RHS, PIECE), F32),
             pltpu.SemaphoreType.DMA((2,)),
             pltpu.SemaphoreType.DMA((2, 16)),
-            pltpu.SemaphoreType.DMA((2,)),
-            pltpu.SemaphoreType.DMA((2,)),
-            pltpu.SemaphoreType.DMA((2,)),
+            pltpu.SemaphoreType.DMA((2, 4)),
+            pltpu.SemaphoreType.DMA((2, 4)),
+            pltpu.SemaphoreType.DMA((2, 4)),
             pltpu.SemaphoreType.DMA((2, 2, BLOCKS)),
             pltpu.SemaphoreType.DMA((2,)),
         ],
@@ -354,6 +412,15 @@
         ),
         name="peec_pair_products",
     )(currents, right_side, geometry)
+    anywhere = pl.BlockSpec(memory_space=pl.ANY)
+    return pl.pallas_call(
+        settle,
+        out_shape=(owned, owned),
+        in_specs=[anywhere, anywhere],
+        out_specs=(anywhere, anywhere),
+        scratch_shapes=[pltpu.SemaphoreType.DMA((2,))],
+        name="settle",
+    )(residual, image)
 
 
 def solution(mesh):

time: 65.4 us -> 66.1 us (1.011)
  Pallas kernels: 62.5 us -> 65.2 us
  local copies, waits for them, and re-layouts: 1.94 us -> 0 us
    pallas_call x0 -> x1, Pallas kernels: none -> 2.11 us  [on_device(): pl.pallas_call(settle, out_shape=(owned, owned), in_specs=[anywhere, anyw...]
    unnamed x4 -> x0, local copies, waits for them, and re-layouts: 1.94 us -> none
where the time goes in v4:
time: 66.1 us; the launch traced here: 65.9 us
  Pallas kernels  65.2 us (99%)
    pallas_call x1, Pallas kernels, on_device(): pl.pallas_call(kernel, out_shape=(owned, owned), in_specs=[vmem, vmem, pl...  63.1 us
    pallas_call x1, Pallas kernels, on_device(): pl.pallas_call(settle, out_shape=(owned, owned), in_specs=[anywhere, anyw...  2.11 us

profile of v4, /device:TPU:1, one launch (start us, length us, event | category | flops | bytes accessed | tf_op | source)
XLA Modules:
  0.0 65.9 jit_solution(7810552318004954401)
XLA Ops:
  0.6 63.1 %peec_pair_products.1 = (f32[16,256]{1,0:T(8,128)}, f32[16,256]{1,0:T(8,128)}) custom-call(bf16[16,1024]{1,0:T(8,128)(2,1)} %cur_ref.1, f32[16,256]{1,0:T(8,128)} %right_ref.1, f32[4,65536]{1,0:T(4,128)} %geo_ref.1), custom_call_target="tpu_custom_call" | custom-call | tf_op jit(solution)/shard_map/peec_pair_products/pallas_call | solution.py:381
  63.8 2.1 %settle.1 = (f32[16,256]{1,0:T(8,128)}, f32[16,256]{1,0:T(8,128)}) custom-call(f32[16,256]{1,0:T(8,128)} %get-tuple-element.4.residual, f32[16,256]{1,0:T(8,128)} %get-tuple-element.5.image), custom_call_target="tpu_custom_call" | custom-call | tf_op jit(solution)/shard_map/settle/pallas_call | solution.py:416

commit v5 on v4

--- a/solution.py
+++ b/solution.py
@@ -315,7 +315,7 @@
             v_ref[1, :, columns] = total if fresh else v_ref[1, :, columns] + total
             return carry
 
-        lax.fori_loop(0, TARGETS // PART, step, 0)
+        lax.fori_loop(0, TARGETS // PART, step, 0, unroll=TARGETS // PART)
 
     take(1, 2)
     sum_chunk(chunk_at(core, 2), True)
@@ -338,8 +338,7 @@
         part_store(1, block, total)
         return carry
 
-    lax.fori_loop(0, BLOCKS, second, 0)
-    img_ref[...] = part_sum(1)
+    lax.fori_loop(0, BLOCKS, second, 0, unroll=2)
 
     for which in range(2):
 
@@ -363,22 +362,13 @@
 
         lax.fori_loop(0, BLOCKS, parted, 0)
 
-
-def settle(residual, image, residual_out, image_out, sems):
-    copies = [
-        pltpu.make_async_copy(residual, residual_out, sems.at[0]),
-        pltpu.make_async_copy(image, image_out, sems.at[1]),
-    ]
-    for copy in copies:
-        copy.start()
-    for copy in copies:
-        copy.wait()
+    img_ref[...] = part_sum(1)
 
 
 def on_device(currents, right_side, geometry):
     vmem = pl.BlockSpec(memory_space=pltpu.VMEM)
     owned = jax.ShapeDtypeStruct((RHS, PIECE), F32)
-    residual, image = pl.pallas_call(
+    return pl.pallas_call(
         kernel,
         out_shape=(owned, owned),
         in_specs=[vmem, vmem, pl.BlockSpec(memory_space=pl.ANY)],
@@ -412,15 +402,6 @@
         ),
         name="peec_pair_products",
     )(currents, right_side, geometry)
-    anywhere = pl.BlockSpec(memory_space=pl.ANY)
-    return pl.pallas_call(
-        settle,
-        out_shape=(owned, owned),
-        in_specs=[anywhere, anywhere],
-        out_specs=(anywhere, anywhere),
-        scratch_shapes=[pltpu.SemaphoreType.DMA((2,))],
-        name="settle",
-    )(residual, image)
 
 
 def solution(mesh):

time: 66.1 us -> 64.2 us (0.971)
  Pallas kernels: 65.2 us -> 61.4 us
  local copies, waits for them, and re-layouts: 0 us -> 1.94 us
    pallas_call x1 -> x0, Pallas kernels: 2.11 us -> none  [on_device(): pl.pallas_call(settle, out_shape=(owned, owned), in_specs=[anywhere, anyw...]
    unnamed x0 -> x4, local copies, waits for them, and re-layouts: none -> 1.94 us
    pallas_call x1, Pallas kernels: 63.1 us -> 61.4 us  [on_device(): pl.pallas_call(kernel, out_shape=(owned, owned), in_specs=[vmem, vmem, pl...]
where the time goes in v5:
time: 64.2 us; the launch traced here: 64 us
  Pallas kernels  61.4 us (96%)
  local copies, waits for them, and re-layouts  1.94 us (3%)
  between operations  0.65 us (1%)
    pallas_call x1, Pallas kernels, on_device(): pl.pallas_call(kernel, out_shape=(owned, owned), in_specs=[vmem, vmem, pl...  61.4 us
    unnamed x4, local copies, waits for them, and re-layouts  1.94 us

profile of v5, /device:TPU:1, one launch (start us, length us, event | category | flops | bytes accessed | tf_op | source)
XLA Modules:
  0.0 64.0 jit_solution(7613512107210368692)
XLA Ops:
  0.6 61.4 %peec_pair_products.1 = (f32[16,256]{1,0:T(8,128)}, f32[16,256]{1,0:T(8,128)}) custom-call(bf16[16,1024]{1,0:T(8,128)(2,1)} %cur_ref.1, f32[16,256]{1,0:T(8,128)} %right_ref.1, f32[4,65536]{1,0:T(4,128)} %geo_ref.1), custom_call_target="tpu_custom_call" | custom-call | tf_op jit(solution)/shard_map/peec_pair_products/pallas_call | solution.py:371
  62.0 0.0 copy-start
  62.0 1.3 %copy.7 = f32[16,256]{1,0:T(8,128)} copy(f32[16,256]{1,0:T(8,128)} %get-tuple-element.4) | data formatting | bytes 32768
  63.4 0.0 copy-done
  63.4 0.6 copy.8
Async XLA Ops:
  62.0 1.3 %copy-start = (f32[16,256]{1,0:T(8,128)S(1)}, f32[16,256]{1,0:T(8,128)}, u32[]{:S(2)}) copy-start(f32[16,256]{1,0:T(8,128)} %get-tuple-element.5) | copy-start | bytes 49156

commit v6 on v5

--- a/solution.py
+++ b/solution.py
@@ -23,7 +23,7 @@
 CHUNK = 256
 SENDERS = 16
 NEAREST = (2, 1, 3, 0)
-FUSED = 3
+FUSED = 4
 
 
 def split3(value):
@@ -54,7 +54,7 @@
 def kernel(
     cur_ref, right_ref, geo_ref, res_ref, img_ref,
     a_ref, b_ref, gs_ref, gt_ref, fs_ref, ft_ref, l_ref, r_ref, zb_ref, yb_ref, zt_ref,
-    own_ref, j_ref, v_ref, p_ref,
+    cur_pair_ref, own_ref, j_ref, v_ref, p_ref,
     geo_sem, gather_send, gather_recv, core_send, core_recv, part_send, part_recv,
 ):
     mirror = lax.axis_index("mirror")
@@ -90,7 +90,16 @@
         greet((k // 8, k % 8 * 8 + across * 2 + core, col))
         return carry
 
+    def along_y(i):
+        other = (mirror * 4 + line + i) % 8
+        return (other // 4, depth * 8 + other % 4 * 2 + core, col), (other // 4 + other % 4) % 2
+
+    def greet_column(i, carry):
+        greet(along_y(i)[0])
+        return carry
+
     sibling = (mirror, row + 1 - 2 * core, col)
+    lax.fori_loop(1, 8, greet_column, 0)
     lax.fori_loop(0, 16, greet_source, 0)
     lax.fori_loop(0, SENDERS, greet_part, 0)
     greet(sibling)
@@ -115,18 +124,42 @@
 
     lax.fori_loop(0, PIECES, source_geo, 0)
     lax.fori_loop(0, BLOCKS, target_geo, 0)
-    own_ref[0] = cur_ref[:, pl.ds(pl.multiple_of(col * PIECE, PIECE), PIECE)]
-
-    def piece_at(which):
+    for half in range(2):
+        cur_pair_ref[half] = cur_ref[:, half * PART : (half + 1) * PART]
+
+    def currents_part():
         rows = pl.ds(pl.multiple_of(mirror * RHS, RHS), RHS)
-        return j_ref.at[which, rows, pl.ds(pl.multiple_of(slot * PIECE, PIECE), PIECE)]
-
-    def gather_copy(which, i):
+        return j_ref.at[0, rows, pl.ds(pl.multiple_of((core * 4 + line) * PART, PART), PART)]
+
+    def currents_copy(i):
+        device, half = along_y(i)
         return pltpu.make_async_remote_copy(
-            src_ref=own_ref.at[which],
-            dst_ref=piece_at(which),
-            send_sem=gather_send.at[which, i],
-            recv_sem=gather_recv.at[which, line],
+            src_ref=cur_pair_ref.at[half],
+            dst_ref=currents_part(),
+            send_sem=gather_send.at[0, i],
+            recv_sem=gather_recv.at[0, line],
+            device_id=device,
+            device_id_type=MESH,
+        )
+
+    def currents_start():
+        def send(i, carry):
+            currents_copy(i).start()
+            return carry
+
+        lax.fori_loop(1, 8, send, 0)
+        pltpu.make_async_copy(cur_pair_ref.at[own_set], currents_part(), gather_recv.at[0, line]).start()
+
+    def piece_at():
+        rows = pl.ds(pl.multiple_of(mirror * RHS, RHS), RHS)
+        return j_ref.at[1, rows, pl.ds(pl.multiple_of(slot * PIECE, PIECE), PIECE)]
+
+    def gather_copy(i):
+        return pltpu.make_async_remote_copy(
+            src_ref=own_ref,
+            dst_ref=piece_at(),
+            send_sem=gather_send.at[1, i],
+            recv_sem=gather_recv.at[1, line],
             device_id=taker(i),
             device_id_type=MESH,
         )
@@ -135,11 +168,11 @@
         other = (line + 2 + i // 4) % 4
         return (home + other) % 2, depth * 8 + other * 2 + core, (col + i) % 4
 
-    def gather_start(which):
+    def gather_start():
         def send(i, carry):
             @pl.when(jnp.logical_not(is_self(*taker(i))))
             def _():
-                gather_copy(which, i).start()
+                gather_copy(i).start()
 
             return carry
 
@@ -147,7 +180,7 @@
 
         @pl.when(home == own_set)
         def _():
-            pltpu.make_async_copy(own_ref.at[which], piece_at(which), gather_recv.at[which, line]).start()
+            pltpu.make_async_copy(own_ref, piece_at(), gather_recv.at[1, line]).start()
 
     def chunk_at(side, away):
         start = side * (SOURCES // 2) + (line + away) % 4 * PART
@@ -197,8 +230,8 @@
             total += p_ref[which, k]
         return total
 
-    pl.semaphore_wait(barrier, jnp.where(home == own_set, 15, 16) + SENDERS + 1)
-    gather_start(0)
+    pl.semaphore_wait(barrier, jnp.where(home == own_set, 15, 16) + SENDERS + 1 + 7)
+    currents_start()
 
     pltpu.make_async_copy(gs_ref, gs_ref, geo_sem.at[0]).wait()
     pltpu.make_async_copy(gt_ref, gt_ref, geo_sem.at[1]).wait()
@@ -298,9 +331,9 @@
     lax.fori_loop(FUSED, BLOCKS, rest, 0)
     residual = right_ref[...] - part_sum(0)
     res_ref[...] = residual
-    own_ref[1] = residual.astype(BF16)
-
-    gather_start(1)
+    own_ref[...] = residual.astype(BF16)
+
+    gather_start()
 
     def product(chunk, columns):
         part = j_ref[1, :, chunk]
@@ -321,11 +354,11 @@
     sum_chunk(chunk_at(core, 2), True)
     take(1, 1)
     sum_chunk(chunk_at(core, 1), False)
+    take(1, 3)
+    take(1, 0)
+    sum_chunk(chunk_at(core, 3), False)
     take_other(1, 2)
     sum_chunk(chunk_at(1 - core, 2), False)
-    take(1, 3)
-    sum_chunk(chunk_at(core, 3), False)
-    take(1, 0)
     for away in (1, 3, 0):
         take_other(1, away)
 
@@ -340,19 +373,24 @@
 
     lax.fori_loop(0, BLOCKS, second, 0, unroll=2)
 
+    def currents_left(i, carry):
+        currents_copy(i).wait_send()
+        return carry
+
+    lax.fori_loop(1, 8, currents_left, 0)
+
+    def gathered(i, carry):
+        @pl.when(jnp.logical_not(is_self(*taker(i))))
+        def _():
+            gather_copy(i).wait_send()
+
+        return carry
+
+    lax.fori_loop(0, 16, gathered, 0)
     for which in range(2):
 
         for away in NEAREST:
             core_copy(which, away).wait_send()
-
-        def gathered(i, carry):
-            @pl.when(jnp.logical_not(is_self(*taker(i))))
-            def _():
-                gather_copy(which, i).wait_send()
-
-            return carry
-
-        lax.fori_loop(0, 16, gathered, 0)
 
         def parted(block, carry):
             for half in range(2):
@@ -385,7 +423,8 @@
             pltpu.VMEM((SOURCES, 128), F32),
             pltpu.VMEM((SOURCES, 128), F32),
             pltpu.VMEM((2, TARGETS), F32),
-            pltpu.VMEM((2, RHS, PIECE), BF16),
+            pltpu.VMEM((2, RHS, PART), BF16),
+            pltpu.VMEM((RHS, PIECE), BF16),
             pltpu.VMEM((2, 2 * RHS, SOURCES), BF16),
             pltpu.VMEM((2, 2 * RHS, TARGETS), F32),
             pltpu.VMEM((2, SENDERS, RHS, PIECE), F32),

time: 64.2 us -> 61.5 us (0.958)
  Pallas kernels: 61.4 us -> 58.6 us
    pallas_call x1, Pallas kernels: 61.4 us -> 58.6 us  [on_device(): pl.pallas_call(kernel, out_shape=(owned, owned), in_specs=[vmem, vmem, pl...]
where the time goes in v6:
time: 61.5 us; the launch traced here: 61.2 us
  Pallas kernels  58.6 us (95%)
  local copies, waits for them, and re-layouts  1.94 us (3%)
  between operations  0.65 us (1%)
    pallas_call x1, Pallas kernels, on_device(): pl.pallas_call(kernel, out_shape=(owned, owned), in_specs=[vmem, vmem, pl...  58.6 us
    unnamed x4, local copies, waits for them, and re-layouts  1.94 us

profile of v6, /device:TPU:1, one launch (start us, length us, event | category | flops | bytes accessed | tf_op | source)
XLA Modules:
  0.0 61.2 jit_solution(64054620235416695)
XLA Ops:
  0.6 58.6 %peec_pair_products.1 = (f32[16,256]{1,0:T(8,128)}, f32[16,256]{1,0:T(8,128)}) custom-call(bf16[16,1024]{1,0:T(8,128)(2,1)} %cur_ref.1, f32[16,256]{1,0:T(8,128)} %right_ref.1, f32[4,65536]{1,0:T(4,128)} %geo_ref.1), custom_call_target="tpu_custom_call" | custom-call | tf_op jit(solution)/shard_map/peec_pair_products/pallas_call | solution.py:409
  59.3 0.0 copy-start
  59.3 1.3 %copy.7 = f32[16,256]{1,0:T(8,128)} copy(f32[16,256]{1,0:T(8,128)} %get-tuple-element.4) | data formatting | bytes 32768
  60.6 0.0 copy-done
  60.6 0.6 copy.8
Async XLA Ops:
  59.3 1.3 %copy-start = (f32[16,256]{1,0:T(8,128)S(1)}, f32[16,256]{1,0:T(8,128)}, u32[]{:S(2)}) copy-start(f32[16,256]{1,0:T(8,128)} %get-tuple-element.5) | copy-start | bytes 49156

commit v7 on v6

--- a/solution.py
+++ b/solution.py
@@ -54,7 +54,7 @@
 def kernel(
     cur_ref, right_ref, geo_ref, res_ref, img_ref,
     a_ref, b_ref, gs_ref, gt_ref, fs_ref, ft_ref, l_ref, r_ref, zb_ref, yb_ref, zt_ref,
-    cur_pair_ref, own_ref, j_ref, v_ref, p_ref,
+    cur_pair_ref, own_ref, j_ref, v_ref, w_ref, p_ref,
     geo_sem, gather_send, gather_recv, core_send, core_recv, part_send, part_recv,
 ):
     mirror = lax.axis_index("mirror")
@@ -209,7 +209,7 @@
     def part_copy(which, half, block):
         start = pl.multiple_of(block * PIECE, PIECE)
         return pltpu.make_async_remote_copy(
-            src_ref=v_ref.at[which, pl.ds(half * RHS, RHS), pl.ds(start, PIECE)],
+            src_ref=w_ref.at[which, pl.ds(half * RHS, RHS), pl.ds(start, PIECE)],
             dst_ref=p_ref.at[which, me],
             send_sem=part_send.at[which, half, block],
             recv_sem=part_recv.at[which],
@@ -219,15 +219,15 @@
 
     def part_store(which, block, total):
         start = pl.multiple_of(block * PIECE, PIECE)
-        v_ref[which, :, pl.ds(start, PIECE)] = total
+        w_ref[which, :, pl.ds(start, PIECE)] = total.astype(BF16)
         for half in range(2):
             part_copy(which, half, block).start()
 
     def part_sum(which):
         pltpu.make_async_copy(p_ref.at[which], p_ref.at[which], part_recv.at[which]).wait()
-        total = p_ref[which, 0]
+        total = p_ref[which, 0].astype(F32)
         for k in range(1, SENDERS):
-            total += p_ref[which, k]
+            total += p_ref[which, k].astype(F32)
         return total
 
     pl.semaphore_wait(barrier, jnp.where(home == own_set, 15, 16) + SENDERS + 1 + 7)
@@ -345,7 +345,7 @@
         def step(i, carry):
             columns = pl.ds(pl.multiple_of(i * PART, PART), PART)
             total = product(chunk, columns)
-            v_ref[1, :, columns] = total if fresh else v_ref[1, :, columns] + total
+            v_ref[:, columns] = total if fresh else v_ref[:, columns] + total
             return carry
 
         lax.fori_loop(0, TARGETS // PART, step, 0, unroll=TARGETS // PART)
@@ -365,7 +365,7 @@
     def second(i, carry):
         block = block_of(i)
         columns = pl.ds(pl.multiple_of(block * PIECE, PIECE), PIECE)
-        total = v_ref[1, :, columns] + product(chunk_at(core, 0), columns)
+        total = v_ref[:, columns] + product(chunk_at(core, 0), columns)
         for away in (1, 3, 0):
             total += product(chunk_at(1 - core, away), columns)
         part_store(1, block, total)
@@ -426,8 +426,9 @@
             pltpu.VMEM((2, RHS, PART), BF16),
             pltpu.VMEM((RHS, PIECE), BF16),
             pltpu.VMEM((2, 2 * RHS, SOURCES), BF16),
-            pltpu.VMEM((2, 2 * RHS, TARGETS), F32),
-            pltpu.VMEM((2, SENDERS, RHS, PIECE), F32),
+            pltpu.VMEM((2 * RHS, TARGETS), F32),
+            pltpu.VMEM((2, 2 * RHS, TARGETS), BF16),
+            pltpu.VMEM((2, SENDERS, RHS, PIECE), BF16),
             pltpu.SemaphoreType.DMA((2,)),
             pltpu.SemaphoreType.DMA((2, 16)),
             pltpu.SemaphoreType.DMA((2, 4)),

time: 61.5 us -> 60.3 us (0.980)
  Pallas kernels: 58.6 us -> 57.5 us
    pallas_call x1, Pallas kernels: 58.6 us -> 57.5 us  [on_device(): pl.pallas_call(kernel, out_shape=(owned, owned), in_specs=[vmem, vmem, pl...]
where the time goes in v7:
time: 60.3 us; the launch traced here: 60 us
  Pallas kernels  57.5 us (95%)
  local copies, waits for them, and re-layouts  1.94 us (3%)
  between operations  0.65 us (1%)
    pallas_call x1, Pallas kernels, on_device(): pl.pallas_call(kernel, out_shape=(owned, owned), in_specs=[vmem, vmem, pl...  57.5 us
    unnamed x4, local copies, waits for them, and re-layouts  1.94 us

profile of v7, /device:TPU:1, one launch (start us, length us, event | category | flops | bytes accessed | tf_op | source)
XLA Modules:
  0.0 60.0 jit_solution(9569167882988536778)
XLA Ops:
  0.6 57.5 %peec_pair_products.1 = (f32[16,256]{1,0:T(8,128)}, f32[16,256]{1,0:T(8,128)}) custom-call(bf16[16,1024]{1,0:T(8,128)(2,1)} %cur_ref.1, f32[16,256]{1,0:T(8,128)} %right_ref.1, f32[4,65536]{1,0:T(4,128)} %geo_ref.1), custom_call_target="tpu_custom_call" | custom-call | tf_op jit(solution)/shard_map/peec_pair_products/pallas_call | solution.py:409
  58.1 0.0 copy-start
  58.1 1.3 %copy.7 = f32[16,256]{1,0:T(8,128)} copy(f32[16,256]{1,0:T(8,128)} %get-tuple-element.4) | data formatting | bytes 32768
  59.4 0.0 copy-done
  59.4 0.6 %copy.8 = f32[16,256]{1,0:T(8,128)} copy(f32[16,256]{1,0:T(8,128)S(1)} %copy-done) | data formatting | bytes 32768
Async XLA Ops:
  58.1 1.3 %copy-start = (f32[16,256]{1,0:T(8,128)S(1)}, f32[16,256]{1,0:T(8,128)}, u32[]{:S(2)}) copy-start(f32[16,256]{1,0:T(8,128)} %get-tuple-element.5) | copy-start | bytes 49156

commit v8 on v7

--- a/solution.py
+++ b/solution.py
@@ -23,7 +23,7 @@
 CHUNK = 256
 SENDERS = 16
 NEAREST = (2, 1, 3, 0)
-FUSED = 4
+FUSED = 3
 
 
 def split3(value):
@@ -52,7 +52,7 @@
 
 
 def kernel(
-    cur_ref, right_ref, geo_ref, res_ref, img_ref,
+    cur_ref, right_ref, geo_ref, out_ref,
     a_ref, b_ref, gs_ref, gt_ref, fs_ref, ft_ref, l_ref, r_ref, zb_ref, yb_ref, zt_ref,
     cur_pair_ref, own_ref, j_ref, v_ref, w_ref, p_ref,
     geo_sem, gather_send, gather_recv, core_send, core_recv, part_send, part_recv,
@@ -105,10 +105,10 @@
     greet(sibling)
 
     def source_geo(k, carry):
-        start = (depth * 8 + (k // 2) % 4 * 2 + k // 8) * 1024 + (own_set * 2 + k % 2) * PIECE
+        start = (depth * 8 + k % 4 * 2 + k // 4) * 1024 + own_set * PART
         pltpu.make_async_copy(
-            geo_ref.at[:, pl.ds(pl.multiple_of(start, PIECE), PIECE)],
-            gs_ref.at[:, pl.ds(pl.multiple_of(k * PIECE, PIECE), PIECE)],
+            geo_ref.at[:, pl.ds(pl.multiple_of(start, PART), PART)],
+            gs_ref.at[:, pl.ds(pl.multiple_of(k * PART, PART), PART)],
             geo_sem.at[0],
         ).start()
         return carry
@@ -122,7 +122,7 @@
         ).start()
         return carry
 
-    lax.fori_loop(0, PIECES, source_geo, 0)
+    lax.fori_loop(0, SOURCES // PART, source_geo, 0)
     lax.fori_loop(0, BLOCKS, target_geo, 0)
     for half in range(2):
         cur_pair_ref[half] = cur_ref[:, half * PART : (half + 1) * PART]
@@ -252,7 +252,7 @@
         yb_ref[at, :] = (jnp.dot(left, pick_y, preferred_element_type=F32) + 0.25) * (4.0 * SQUARE)
         return carry
 
-    lax.fori_loop(0, SOURCES // 512, spread, 0)
+    lax.fori_loop(0, SOURCES // 512, spread, 0, unroll=SOURCES // 512)
 
     def make_tile(at, block):
         start = pl.multiple_of(block * PIECE, PIECE)
@@ -330,7 +330,7 @@
 
     lax.fori_loop(FUSED, BLOCKS, rest, 0)
     residual = right_ref[...] - part_sum(0)
-    res_ref[...] = residual
+    out_ref[0:RHS] = residual
     own_ref[...] = residual.astype(BF16)
 
     gather_start()
@@ -359,19 +359,22 @@
     sum_chunk(chunk_at(core, 3), False)
     take_other(1, 2)
     sum_chunk(chunk_at(1 - core, 2), False)
-    for away in (1, 3, 0):
+    sum_chunk(chunk_at(core, 0), False)
+    take_other(1, 1)
+    sum_chunk(chunk_at(1 - core, 1), False)
+    for away in (3, 0):
         take_other(1, away)
 
     def second(i, carry):
         block = block_of(i)
         columns = pl.ds(pl.multiple_of(block * PIECE, PIECE), PIECE)
-        total = v_ref[:, columns] + product(chunk_at(core, 0), columns)
-        for away in (1, 3, 0):
+        total = v_ref[:, columns]
+        for away in (3, 0):
             total += product(chunk_at(1 - core, away), columns)
         part_store(1, block, total)
         return carry
 
-    lax.fori_loop(0, BLOCKS, second, 0, unroll=2)
+    lax.fori_loop(0, BLOCKS, second, 0, unroll=4)
 
     def currents_left(i, carry):
         currents_copy(i).wait_send()
@@ -400,17 +403,16 @@
 
         lax.fori_loop(0, BLOCKS, parted, 0)
 
-    img_ref[...] = part_sum(1)
+    out_ref[RHS : 2 * RHS] = part_sum(1)
 
 
 def on_device(currents, right_side, geometry):
     vmem = pl.BlockSpec(memory_space=pltpu.VMEM)
-    owned = jax.ShapeDtypeStruct((RHS, PIECE), F32)
-    return pl.pallas_call(
+    both = pl.pallas_call(
         kernel,
-        out_shape=(owned, owned),
+        out_shape=jax.ShapeDtypeStruct((2 * RHS, PIECE), F32),
         in_specs=[vmem, vmem, pl.BlockSpec(memory_space=pl.ANY)],
-        out_specs=(vmem, vmem),
+        out_specs=vmem,
         scratch_shapes=[
             pltpu.VMEM((SOURCES, TARGETS), BF16),
             pltpu.VMEM((SOURCES, TARGETS), BF16),
@@ -442,6 +444,7 @@
         ),
         name="peec_pair_products",
     )(currents, right_side, geometry)
+    return both[:RHS], both[RHS:]
 
 
 def solution(mesh):

time: 60.3 us -> 58.9 us (0.977)
  Pallas kernels: 57.5 us -> 56.6 us
    unnamed x4 -> x0, local copies, waits for them, and re-layouts: 1.94 us -> none
    slice x0 -> x1, local copies, waits for them, and re-layouts: none -> 1.35 us  [on_device(): return (both[:RHS], both[RHS:])]
    pallas_call x1, Pallas kernels: 57.5 us -> 56.6 us  [on_device(): pl.pallas_call(kernel, out_shape=jax.ShapeDtypeStruct((2 * RHS, PIECE), F...]
where the time goes in v8:
time: 58.9 us; the launch traced here: 58.6 us
  Pallas kernels  56.6 us (96%)
  local copies, waits for them, and re-layouts  1.35 us (2%)
  between operations  0.64 us (1%)
    pallas_call x1, Pallas kernels, on_device(): pl.pallas_call(kernel, out_shape=jax.ShapeDtypeStruct((2 * RHS, PIECE), F...  56.6 us
    slice x1, local copies, waits for them, and re-layouts, on_device(): return (both[:RHS], both[RHS:])  1.35 us

profile of v8, /device:TPU:1, one launch (start us, length us, event | category | flops | bytes accessed | tf_op | source)
XLA Modules:
  0.0 58.6 jit_solution(12804508169259336688)
XLA Ops:
  0.6 56.6 %peec_pair_products.1 = f32[32,256]{1,0:T(8,128)} custom-call(bf16[16,1024]{1,0:T(8,128)(2,1)} %cur_ref.1, f32[16,256]{1,0:T(8,128)} %right_ref.1, f32[4,65536]{1,0:T(4,128)} %geo_ref.1), custom_call_target="tpu_custom_call" | custom-call | tf_op jit(solution)/shard_map/peec_pair_products/pallas_call | solution.py:411
  57.2 1.3 %fusion = (f32[16,256]{1,0:T(8,128)}, f32[16,256]{1,0:T(8,128)}) fusion(f32[32,256]{1,0:T(8,128)} %peec_pair_products.1), kind=kLoop, calls=%fused_computation | loop fusion | bytes 65536 | tf_op jit(solution)/shard_map/slice | solution.py:447

commit v9 on v8

--- a/solution.py
+++ b/solution.py
@@ -23,6 +23,7 @@
 CHUNK = 256
 SENDERS = 16
 NEAREST = (2, 1, 3, 0)
+EARLY = 2
 FUSED = 3
 
 
@@ -230,9 +231,6 @@
             total += p_ref[which, k].astype(F32)
         return total
 
-    pl.semaphore_wait(barrier, jnp.where(home == own_set, 15, 16) + SENDERS + 1 + 7)
-    currents_start()
-
     pltpu.make_async_copy(gs_ref, gs_ref, geo_sem.at[0]).wait()
     pltpu.make_async_copy(gt_ref, gt_ref, geo_sem.at[1]).wait()
     store_terms(gs_ref, fs_ref, True)
@@ -312,7 +310,14 @@
 
         return carry
 
-    lax.fori_loop(FUSED, BLOCKS, hand_over, 0)
+    def ahead(i, carry):
+        build(block_of(i))
+        return carry
+
+    lax.fori_loop(FUSED, FUSED + EARLY, ahead, 0)
+    pl.semaphore_wait(barrier, jnp.where(home == own_set, 15, 16) + SENDERS + 1 + 7)
+    currents_start()
+    lax.fori_loop(FUSED + EARLY, BLOCKS, hand_over, 0)
     for away in NEAREST:
         take_other(0, away)
 

time: 58.9 us -> 59.7 us (1.014)
  Pallas kernels: 56.6 us -> 57.4 us
    pallas_call x1, Pallas kernels: 56.6 us -> 57.4 us  [on_device(): pl.pallas_call(kernel, out_shape=jax.ShapeDtypeStruct((2 * RHS, PIECE), F...]
where the time goes in v9:
time: 59.7 us; the launch traced here: 59.4 us
  Pallas kernels  57.4 us (96%)
  local copies, waits for them, and re-layouts  1.35 us (2%)
  between operations  0.64 us (1%)
    pallas_call x1, Pallas kernels, on_device(): pl.pallas_call(kernel, out_shape=jax.ShapeDtypeStruct((2 * RHS, PIECE), F...  57.4 us
    slice x1, local copies, waits for them, and re-layouts, on_device(): return (both[:RHS], both[RHS:])  1.35 us

profile of v9, /device:TPU:1, one launch (start us, length us, event | category | flops | bytes accessed | tf_op | source)
XLA Modules:
  0.0 59.4 jit_solution(3377008034085260976)
XLA Ops:
  0.6 57.4 %peec_pair_products.1 = f32[32,256]{1,0:T(8,128)} custom-call(bf16[16,1024]{1,0:T(8,128)(2,1)} %cur_ref.1, f32[16,256]{1,0:T(8,128)} %right_ref.1, f32[4,65536]{1,0:T(4,128)} %geo_ref.1), custom_call_target="tpu_custom_call" | custom-call | tf_op jit(solution)/shard_map/peec_pair_products/pallas_call | solution.py:416
  58.0 1.3 %fusion = (f32[16,256]{1,0:T(8,128)}, f32[16,256]{1,0:T(8,128)}) fusion(f32[32,256]{1,0:T(8,128)} %peec_pair_products.1), kind=kLoop, calls=%fused_computation | loop fusion | bytes 65536 | tf_op jit(solution)/shard_map/slice | solution.py:452

commit v10 on v8

--- a/solution.py
+++ b/solution.py
@@ -230,9 +230,6 @@
             total += p_ref[which, k].astype(F32)
         return total
 
-    pl.semaphore_wait(barrier, jnp.where(home == own_set, 15, 16) + SENDERS + 1 + 7)
-    currents_start()
-
     pltpu.make_async_copy(gs_ref, gs_ref, geo_sem.at[0]).wait()
     pltpu.make_async_copy(gt_ref, gt_ref, geo_sem.at[1]).wait()
     store_terms(gs_ref, fs_ref, True)
@@ -312,6 +309,8 @@
 
         return carry
 
+    pl.semaphore_wait(barrier, jnp.where(home == own_set, 15, 16) + SENDERS + 1 + 7)
+    currents_start()
     lax.fori_loop(FUSED, BLOCKS, hand_over, 0)
     for away in NEAREST:
         take_other(0, away)

time: 58.9 us -> 58.2 us (0.988)
  Pallas kernels: 56.6 us -> 55.9 us
    pallas_call x1, Pallas kernels: 56.6 us -> 55.9 us  [on_device(): pl.pallas_call(kernel, out_shape=jax.ShapeDtypeStruct((2 * RHS, PIECE), F...]
where the time goes in v10:
time: 58.2 us; the launch traced here: 57.9 us
  Pallas kernels  55.9 us (96%)
  local copies, waits for them, and re-layouts  1.35 us (2%)
  between operations  0.64 us (1%)
    pallas_call x1, Pallas kernels, on_device(): pl.pallas_call(kernel, out_shape=jax.ShapeDtypeStruct((2 * RHS, PIECE), F...  55.9 us
    slice x1, local copies, waits for them, and re-layouts, on_device(): return (both[:RHS], both[RHS:])  1.35 us

profile of v10, /device:TPU:1, one launch (start us, length us, event | category | flops | bytes accessed | tf_op | source)
XLA Modules:
  0.0 57.9 jit_solution(7524224345543557414)
XLA Ops:
  0.6 55.9 %peec_pair_products.1 = f32[32,256]{1,0:T(8,128)} custom-call(bf16[16,1024]{1,0:T(8,128)(2,1)} %cur_ref.1, f32[16,256]{1,0:T(8,128)} %right_ref.1, f32[4,65536]{1,0:T(4,128)} %geo_ref.1), custom_call_target="tpu_custom_call" | custom-call | tf_op jit(solution)/shard_map/peec_pair_products/pallas_call | solution.py:410
  56.5 1.3 %fusion = (f32[16,256]{1,0:T(8,128)}, f32[16,256]{1,0:T(8,128)}) fusion(f32[32,256]{1,0:T(8,128)} %peec_pair_products.1), kind=kLoop, calls=%fused_computation | loop fusion | bytes 65536 | tf_op jit(solution)/shard_map/slice | solution.py:446

commit v11 on v10

--- a/solution.py
+++ b/solution.py
@@ -23,7 +23,7 @@
 CHUNK = 256
 SENDERS = 16
 NEAREST = (2, 1, 3, 0)
-FUSED = 3
+FUSED = 4
 
 
 def split3(value):

time: 58.2 us -> 58.7 us (level)
  no operation moved by 1% of the time
where the time goes in v11:
time: 58.7 us; the launch traced here: 58.2 us
  Pallas kernels  56.2 us (96%)
  local copies, waits for them, and re-layouts  1.35 us (2%)
  between operations  0.64 us (1%)
    pallas_call x1, Pallas kernels, on_device(): pl.pallas_call(kernel, out_shape=jax.ShapeDtypeStruct((2 * RHS, PIECE), F...  56.2 us
    slice x1, local copies, waits for them, and re-layouts, on_device(): return (both[:RHS], both[RHS:])  1.35 us

profile of v11, /device:TPU:1, one launch (start us, length us, event | category | flops | bytes accessed | tf_op | source)
XLA Modules:
  0.0 58.2 jit_solution(3122883574885434083)
XLA Ops:
  0.6 56.2 %peec_pair_products.1 = f32[32,256]{1,0:T(8,128)} custom-call(bf16[16,1024]{1,0:T(8,128)(2,1)} %cur_ref.1, f32[16,256]{1,0:T(8,128)} %right_ref.1, f32[4,65536]{1,0:T(4,128)} %geo_ref.1), custom_call_target="tpu_custom_call" | custom-call | tf_op jit(solution)/shard_map/peec_pair_products/pallas_call | solution.py:410
  56.9 1.3 %fusion = (f32[16,256]{1,0:T(8,128)}, f32[16,256]{1,0:T(8,128)}) fusion(f32[32,256]{1,0:T(8,128)} %peec_pair_products.1), kind=kLoop, calls=%fused_computation | loop fusion | bytes 65536 | tf_op jit(solution)/shard_map/slice | solution.py:446
